TPU v7x, 32 devices: a whole 2x2x4 slice. The times are simulated.
32 devices in a mesh: scene: 4 (over x, core), brick: 8 (over z, y).
Axes of the slice: x: 2, y: 2, z: 4, core: 2. Of those that a mesh axis runs over, the one named last changes fastest.
Arguments:
- features: bfloat16 [4, 4096, 64], P('scene', 'brick'), may hold values from -6 to 6
- cotangent: bfloat16 [4, 4096, 64], P('scene', 'brick'), may hold values from -6 to 6
- first_weight: bfloat16 [1728, 64], replicated, may hold values from -0.15625 to 0.15625
- second_weight: bfloat16 [1728, 64], replicated, may hold values from -0.15625 to 0.15625
- send_rows: int32 [4, 1024], P('scene', 'brick'), may hold values from 0 to 512, as said below
- gather_rows: int32 [4, 8000], P('scene', 'brick'), may hold values from 0 to 640, as said below
Outputs:
- output: bfloat16 [4, 4096, 64], P('scene', 'brick')
- grad_input: bfloat16 [4, 4096, 64], P('scene', 'brick')
- grad_first: float32 [1728, 64], replicated
- grad_second: float32 [1728, 64], replicated
Inputs may be any that keep to these rules, and one draw needn't show every extreme that they name: `send_rows`: entries equal to 512 are empty slots; used entries come first in each half and name voxels on the face of active bricks towards that neighbour; in every draw some pair of neighbouring indices sends all 64 rows to each other. Index 0 sends nothing down, the last index nothing up. `gather_rows`: row 640 is the zero row; inactive slots read only it; rows 512 and up read boundary rows in the order of the neighbour's send list. Every index of brick holds exactly one active brick slot, and bricks touch only bricks of the same or an adjacent index.
All inputs are finite; a program needn't handle non-finite values.
Results may differ from a plain program's by a relative error of at most 0.0059.
Values may be sent and summed in bfloat16 or wider, within the bound.
No kernel may reach another device: no remote copies, remote signals or barrier semaphores. Data moves between devices by JAX's collectives and lax.ppermute only.
A program may use at most 64 MiB of HBM per device.

v0:
```python
import jax
import jax.numpy as jnp
from jax import lax
from jax.sharding import PartitionSpec as P

EDGE = 8
VOX = 512


def extended(block, sides, width):
    for axis, dim in sides:
        count = lax.axis_size(axis)
        forward = [(i, i + 1) for i in range(count - 1)]
        backward = [(target, source) for source, target in forward]
        low = lax.ppermute(
            lax.slice_in_dim(block, block.shape[dim] - width, None, axis=dim), axis, forward
        )
        high = lax.ppermute(lax.slice_in_dim(block, 0, width, axis=dim), axis, backward)
        block = jnp.concatenate([low, block, high], axis=dim)
    return block


def silu_slope(values):
    sig = jax.nn.sigmoid(values)
    return sig * (1.0 + values * (1.0 - sig))


def outgoing_rows(values, send_list):
    zero_row = jnp.zeros((1, values.shape[1]), values.dtype)
    return jnp.take(jnp.concatenate([values, zero_row], axis=0), send_list, axis=0)


def assemble(values, arrived, gather_list, slot_width):
    zero_row = jnp.zeros((1, values.shape[1]), values.dtype)
    pool = jnp.concatenate(
        [values, arrived[:slot_width], arrived[3 * slot_width :], zero_row], axis=0
    )
    return jnp.take(pool, gather_list, axis=0).reshape(
        -1, EDGE + 2, EDGE + 2, EDGE + 2, values.shape[1]
    )


def window_rows(padded, row_off, col_off, extent):
    slabs = [
        padded[:, row_off : row_off + extent, col_off : col_off + extent, depth : depth + extent, :]
        for depth in range(3)
    ]
    return jnp.concatenate(slabs, axis=-1).reshape(-1, 3 * padded.shape[-1])


def convolve(padded, weight, extent):
    width = padded.shape[-1]
    accumulated = jnp.zeros((padded.shape[0] * extent**3, weight.shape[1]), jnp.float32)
    for row_off in range(3):
        for col_off in range(3):
            start = (row_off * 3 + col_off) * 3 * width
            accumulated = accumulated + jnp.dot(
                window_rows(padded, row_off, col_off, extent),
                weight[start : start + 3 * width],
                preferred_element_type=jnp.float32,
            )
    return accumulated


def weight_gradient(padded, delta_rows):
    pieces = []
    for row_off in range(3):
        for col_off in range(3):
            pieces.append(
                lax.dot_general(
                    window_rows(padded, row_off, col_off, EDGE),
                    delta_rows,
                    (((0,), (0,)), ((), ())),
                    preferred_element_type=jnp.float32,
                )
            )
    return jnp.concatenate(pieces, axis=0)


def flipped(weight):
    width = weight.shape[1]
    return jnp.transpose(weight.reshape(27, width, width)[::-1], (0, 2, 1)).reshape(
        27 * width, width
    )


def shards(features, cotangent, first_weight, second_weight, send_rows, gather_rows):
    local_feat = features[0]
    local_cot = cotangent[0]
    send_list = send_rows[0]
    gather_list = gather_rows[0]
    slot_width = send_list.shape[0] // 2

    def forward_pad(values):
        arrived = extended(outgoing_rows(values, send_list), (("brick", 0),), slot_width)
        return assemble(values, arrived, gather_list, slot_width)

    def delta_pad(values):
        arrived = extended(outgoing_rows(values, send_list), (("brick", 0),), slot_width)
        return assemble(values, arrived, gather_list, slot_width)

    padded_input = forward_pad(local_feat)
    first_pre = convolve(padded_input, first_weight, EDGE)
    first_act = (first_pre * jax.nn.sigmoid(first_pre)).astype(jnp.bfloat16)
    padded_act = forward_pad(first_act)
    second_pre = convolve(padded_act, second_weight, EDGE)
    output = (second_pre * jax.nn.sigmoid(second_pre)).astype(jnp.bfloat16)
    second_delta = (local_cot.astype(jnp.float32) * silu_slope(second_pre)).astype(jnp.bfloat16)
    grad_second = weight_gradient(padded_act, second_delta)
    first_back = convolve(delta_pad(second_delta), flipped(second_weight), EDGE)
    first_delta = (first_back * silu_slope(first_pre)).astype(jnp.bfloat16)
    grad_first = weight_gradient(padded_input, first_delta)
    input_back = convolve(delta_pad(first_delta), flipped(first_weight), EDGE)
    grad_input = input_back.astype(jnp.bfloat16)
    grad_first, grad_second = lax.psum((grad_first, grad_second), ("scene", "brick"))
    grad_scale = float(lax.axis_size("scene") * lax.axis_size("brick") * VOX) ** (-0.5)
    return (output[None], grad_input[None], grad_first * grad_scale, grad_second * grad_scale)


def solution(mesh):
    in_specs = (
        P("scene", "brick", None),
        P("scene", "brick", None),
        P(),
        P(),
        P("scene", "brick"),
        P("scene", "brick"),
    )
    out_specs = (P("scene", "brick", None), P("scene", "brick", None), P(), P())
    return jax.shard_map(shards, mesh=mesh, in_specs=in_specs, out_specs=out_specs, check_vma=False)
```

profile of v0, /device:TPU:0, one launch (start us, length us, event | category | flops | bytes accessed | tf_op | source)
XLA Modules:
  0.0 242.3 jit_solution(8681243821451557241)
XLA Ops:
  7.9 1.0 copy.21
  9.8 4.9 %collective-permute-start = (bf16[64,64]{1,0:T(8,128)(2,1)S(1)}, bf16[64,64]{1,0:T(8,128)(2,1)S(1)}, u32[]{:S(2)}, u32[]{:S(2)}) collective-permute-start(bf16[64,64]{1,0:T(8,128)(2,1)S(1)} %get-tuple-element.136), channel_id=1, source_target_pairs={{0,1},{1,2},{2,3},{3,4},{4,5},{5,6},{6,7},{8,9},{9,10},{10,11},{11... | collective-permute-start | bytes 24584 | tf_op jit(solution)/shard_map/ppermute | solution.py:15
  14.7 1.3 collective-permute-start.1
  17.1 1.0 fusion.27
  19.2 1.2 collective-permute-done.1
  20.5 3.3 %gather_fusion.1 = bf16[1000,64]{1,0:T(8,128)(2,1)S(1)} fusion(bf16[641,64]{1,0:T(8,128)(2,1)S(1)} %maximum_maximum_fusion, s32[1024]{0:T(1024)S(1)} %pad_clamp_fusion), kind=kCustom, calls=%fused_computation.1.clone | custom fusion | bytes 260000 | tf_op jit(solution)/shard_map/jit(_take)/gather | solution.py:38
  27.6 0.9 multiply_convert_fusion.1
  28.7 0.8 gather_fusion.2
  30.2 4.3 %collective-permute-start.2 = (bf16[64,64]{0,1:T(8,128)(2,1)S(1)}, bf16[64,64]{0,1:T(8,128)(2,1)S(1)}, u32[]{:S(2)}, u32[]{:S(2)}) collective-permute-start(bf16[64,64]{0,1:T(8,128)(2,1)S(1)} %get-tuple-element.142), channel_id=1, source_target_pairs={{0,1},{1,2},{2,3},{3,4},{4,5},{5,6},{6,7},{8,9},{9,10},{10,11},{11... | collective-permute-start | bytes 24584 | tf_op jit(solution)/shard_map/ppermute | solution.py:15
  34.6 1.3 collective-permute-start.3
  48.8 3.3 %gather_fusion.3 = bf16[1000,64]{1,0:T(8,128)(2,1)S(1)} fusion(bf16[641,64]{1,0:T(8,128)(2,1)S(1)} %copy.25, s32[1024]{0:T(1024)S(1)} %copy-done.30), kind=kCustom, calls=%fused_computation.5.clone | custom fusion | bytes 260000 | tf_op jit(solution)/shard_map/jit(_take)/gather | solution.py:38
  54.1 1.0 convolution_add_fusion.22
  55.2 1.0 convolution_add_fusion.21
  56.4 1.0 convolution_add_fusion.20
  57.5 1.0 convolution_add_fusion.19
  58.7 1.0 convolution_add_fusion.18
  59.8 1.0 convolution_add_fusion.17
  61.6 0.9 fusion.4
  64.1 0.8 gather_fusion.4
  65.7 4.5 %collective-permute-start.4 = (bf16[64,64]{0,1:T(8,128)(2,1)S(1)}, bf16[64,64]{0,1:T(8,128)(2,1)S(1)}, u32[]{:S(2)}, u32[]{:S(2)}) collective-permute-start(bf16[64,64]{0,1:T(8,128)(2,1)S(1)} %get-tuple-element.140), channel_id=1, source_target_pairs={{0,1},{1,2},{2,3},{3,4},{4,5},{5,6},{6,7},{8,9},{9,10},{10,11},{11... | collective-permute-start | bytes 24584 | tf_op jit(solution)/shard_map/ppermute | solution.py:15
  70.2 1.5 collective-permute-start.5
  71.9 0.9 concatenate.201
  72.8 3.8 %collective-permute-done.5 = bf16[64,64]{0,1:T(8,128)(2,1)S(1)} collective-permute-done((bf16[64,64]{0,1:T(8,128)(2,1)S(1)}, bf16[64,64]{0,1:T(8,128)(2,1)S(1)}, u32[]{:S(2)}, u32[]{:S(2)}) %collective-permute-start.5) | collective-permute-done | bytes 8224 | tf_op jit(solution)/shard_map/ppermute | solution.py:18
  76.9 3.3 %gather_fusion.5 = bf16[1000,64]{1,0:T(8,128)(2,1)S(1)} fusion(bf16[641,64]{1,0:T(8,128)(2,1)S(1)} %copy.28, s32[1024]{0:T(1024)S(1)} %copy-done.30), kind=kCustom, calls=%fused_computation.6.clone | custom fusion | bytes 260000 | tf_op jit(solution)/shard_map/jit(_take)/gather | solution.py:38
  93.3 4.8 %collective-permute-start.6 = (bf16[64,64]{0,1:T(8,128)(2,1)S(1)}, bf16[64,64]{0,1:T(8,128)(2,1)S(1)}, u32[]{:S(2)}, u32[]{:S(2)}) collective-permute-start(bf16[64,64]{0,1:T(8,128)(2,1)S(1)} %get-tuple-element.138), channel_id=1, source_target_pairs={{0,1},{1,2},{2,3},{3,4},{4,5},{5,6},{6,7},{8,9},{9,10},{10,11},{11... | collective-permute-start | bytes 24584 | tf_op jit(solution)/shard_map/ppermute | solution.py:15
  98.1 1.3 collective-permute-start.7
  99.6 0.9 concatenate.200
  100.5 3.2 %collective-permute-done.7 = bf16[64,64]{0,1:T(8,128)(2,1)S(1)} collective-permute-done((bf16[64,64]{0,1:T(8,128)(2,1)S(1)}, bf16[64,64]{0,1:T(8,128)(2,1)S(1)}, u32[]{:S(2)}, u32[]{:S(2)}) %collective-permute-start.7) | collective-permute-done | bytes 8224 | tf_op jit(solution)/shard_map/ppermute | solution.py:18
  104.0 3.3 %gather_fusion.7 = bf16[1000,64]{1,0:T(8,128)(2,1)S(1)} fusion(bf16[641,64]{1,0:T(8,128)(2,1)S(1)} %copy.40, s32[1024]{0:T(1024)S(1)} %copy-done.30), kind=kCustom, calls=%fused_computation.7.clone | custom fusion | bytes 260000 | tf_op jit(solution)/shard_map/jit(_take)/gather | solution.py:38
  116.3 0.8 fusion.3
  117.1 115.6 %all-reduce.7.cloned.1.call-done = (f32[1728,64]{0,1:T(8,128)}, f32[1728,64]{0,1:T(8,128)}) async-done(((f32[1728,64]{0,1:T(8,128)}, f32[1728,64]{0,1:T(8,128)}), (f32[1728,64]{0,1:T(8,128)}, f32[1728,64]{0,1:T(8,128)})) %all-reduce.7.cloned.1.call-update) | async-done | bytes 884752 | tf_op jit(solution)/shard_map/psum | solution.py:115
  232.7 1.9 broadcast_multiply_fusion
  (246 shorter events, 50.4 us)
Async XLA Ops:
  7.2 225.6 %all-reduce.7.cloned.1.call-start = ((), (), s32[]{:S(2)}) async-start(), calls=%async_computation | async-start | bytes 1835008 | tf_op jit(solution)/shard_map/psum | solution.py:115
  7.9 1.8 copy-start.38
  7.9 1.0 copy-start.37
  9.0 7.1 %copy-start.1 = (bf16[1728,64]{0,1:T(8,128)(2,1)S(1)}, bf16[1728,64]{0,1:T(8,128)(2,1)}, u32[]{:S(2)}) copy-start(bf16[1728,64]{0,1:T(8,128)(2,1)} %param.13) | copy-start | bytes 663556
  9.8 6.2 %copy-start.36 = (s32[1,1000]{1,0:T(1,128)S(1)}, s32[1,1000]{1,0:T(1,128)}, u32[]{:S(2)}) copy-start(s32[1,1000]{1,0:T(1,128)} %param.15) | copy-start | bytes 12004
  9.8 9.4 %collective-permute-start = (bf16[64,64]{1,0:T(8,128)(2,1)S(1)}, bf16[64,64]{1,0:T(8,128)(2,1)S(1)}, u32[]{:S(2)}, u32[]{:S(2)}) collective-permute-start(bf16[64,64]{1,0:T(8,128)(2,1)S(1)} %get-tuple-element.136), channel_id=1, source_target_pairs={{0,1},{1,2},{2,3},{3,4},{4,5},{5,6},{6,7},{8,9},{9,10},{10,11},{11... | collective-permute-start | bytes 24584 | tf_op jit(solution)/shard_map/ppermute | solution.py:15
  14.7 5.6 %collective-permute-start.1 = (bf16[64,64]{1,0:T(8,128)(2,1)S(1)}, bf16[64,64]{1,0:T(8,128)(2,1)S(1)}, u32[]{:S(2)}, u32[]{:S(2)}) collective-permute-start(bf16[64,64]{1,0:T(8,128)(2,1)S(1)} %get-tuple-element.137), channel_id=1, source_target_pairs={{1,0},{2,1},{3,2},{4,3},{5,4},{6,5},{7,6},{9,8},{10,9},{11,10},{12... | collective-permute-start | bytes 24584 | tf_op jit(solution)/shard_map/ppermute | solution.py:18
  16.1 7.8 %copy-start.34 = (pred[1000]{0:T(1024)(128)(4,1)}, pred[1000]{0:T(1024)(128)(4,1)S(1)}, u32[]{:S(2)}) copy-start(pred[1000]{0:T(1024)(128)(4,1)S(1)} %compare_and_fusion) | copy-start | bytes 3004
  17.1 1.0 copy-start
  18.1 2.4 copy-start.29
  19.2 1.4 copy-start.31
  27.6 0.9 copy-start.2
  30.2 17.8 %collective-permute-start.2 = (bf16[64,64]{0,1:T(8,128)(2,1)S(1)}, bf16[64,64]{0,1:T(8,128)(2,1)S(1)}, u32[]{:S(2)}, u32[]{:S(2)}) collective-permute-start(bf16[64,64]{0,1:T(8,128)(2,1)S(1)} %get-tuple-element.142), channel_id=1, source_target_pairs={{0,1},{1,2},{2,3},{3,4},{4,5},{5,6},{6,7},{8,9},{9,10},{10,11},{11... | collective-permute-start | bytes 24584 | tf_op jit(solution)/shard_map/ppermute | solution.py:15
  34.6 13.5 %collective-permute-start.3 = (bf16[64,64]{0,1:T(8,128)(2,1)S(1)}, bf16[64,64]{0,1:T(8,128)(2,1)S(1)}, u32[]{:S(2)}, u32[]{:S(2)}) collective-permute-start(bf16[64,64]{0,1:T(8,128)(2,1)S(1)} %get-tuple-element.143), channel_id=1, source_target_pairs={{1,0},{2,1},{3,2},{4,3},{5,4},{6,5},{7,6},{9,8},{10,9},{11,10},{12... | collective-permute-start | bytes 24584 | tf_op jit(solution)/shard_map/ppermute | solution.py:18
  35.9 0.8 copy-start.12
  36.1 1.2 copy-start.11
  37.3 0.9 copy-start.10
  37.9 0.9 copy-start.9
  38.8 0.9 copy-start.8
  39.4 0.9 copy-start.7
  40.3 0.9 copy-start.6
  40.9 0.9 copy-start.5
  48.8 3.3 %copy-start.35 = (pred[1000]{0:T(1024)(128)(4,1)S(1)}, pred[1000]{0:T(1024)(128)(4,1)}, u32[]{:S(2)}) copy-start(pred[1000]{0:T(1024)(128)(4,1)} %copy-done.34) | copy-start | bytes 3004
  60.8 0.8 copy-start.41
  65.7 7.1 %collective-permute-start.4 = (bf16[64,64]{0,1:T(8,128)(2,1)S(1)}, bf16[64,64]{0,1:T(8,128)(2,1)S(1)}, u32[]{:S(2)}, u32[]{:S(2)}) collective-permute-start(bf16[64,64]{0,1:T(8,128)(2,1)S(1)} %get-tuple-element.140), channel_id=1, source_target_pairs={{0,1},{1,2},{2,3},{3,4},{4,5},{5,6},{6,7},{8,9},{9,10},{10,11},{11... | collective-permute-start | bytes 24584 | tf_op jit(solution)/shard_map/ppermute | solution.py:15
  70.2 6.4 %collective-permute-start.5 = (bf16[64,64]{0,1:T(8,128)(2,1)S(1)}, bf16[64,64]{0,1:T(8,128)(2,1)S(1)}, u32[]{:S(2)}, u32[]{:S(2)}) collective-permute-start(bf16[64,64]{0,1:T(8,128)(2,1)S(1)} %get-tuple-element.141), channel_id=1, source_target_pairs={{1,0},{2,1},{3,2},{4,3},{5,4},{6,5},{7,6},{9,8},{10,9},{11,10},{12... | collective-permute-start | bytes 24584 | tf_op jit(solution)/shard_map/ppermute | solution.py:18
  88.8 0.9 copy-start.43
  89.8 0.9 copy-start.3
  93.3 7.2 %collective-permute-start.6 = (bf16[64,64]{0,1:T(8,128)(2,1)S(1)}, bf16[64,64]{0,1:T(8,128)(2,1)S(1)}, u32[]{:S(2)}, u32[]{:S(2)}) collective-permute-start(bf16[64,64]{0,1:T(8,128)(2,1)S(1)} %get-tuple-element.138), channel_id=1, source_target_pairs={{0,1},{1,2},{2,3},{3,4},{4,5},{5,6},{6,7},{8,9},{9,10},{10,11},{11... | collective-permute-start | bytes 24584 | tf_op jit(solution)/shard_map/ppermute | solution.py:15
  98.1 5.6 %collective-permute-start.7 = (bf16[64,64]{0,1:T(8,128)(2,1)S(1)}, bf16[64,64]{0,1:T(8,128)(2,1)S(1)}, u32[]{:S(2)}, u32[]{:S(2)}) collective-permute-start(bf16[64,64]{0,1:T(8,128)(2,1)S(1)} %get-tuple-element.139), channel_id=1, source_target_pairs={{1,0},{2,1},{3,2},{4,3},{5,4},{6,5},{7,6},{9,8},{10,9},{11,10},{12... | collective-permute-start | bytes 24584 | tf_op jit(solution)/shard_map/ppermute | solution.py:18
  115.5 0.8 copy-start.28
  232.7 1.9 copy-start.4
  (21 other events, 16.2 us)
Sparse Core Ops, SparseCore 0:
  100.7 132.0 all-reduce.6
where the time goes:
time: 244 us; the launch traced here: 242 us
  waiting for transfers between devices  124 us (51%)
  local copies, waits for them, and re-layouts  52.4 us (21%)
  starting transfers between devices  23.9 us (10%)
  matrix products  17.2 us (7%)
  between operations  15 us (6%)
  other arithmetic  9.84 us (4%)
    psum x1, waiting for transfers between devices, shards(): lax.psum((grad_first, grad_second), ('scene', 'brick'))  116 us
    ppermute x4, starting transfers between devices, extended(): lax.ppermute(lax.slice_in_dim(block, block.shape[dim] - width, None, axis...  18.6 us
    unnamed x92, local copies, waits for them, and re-layouts  16.1 us
    dot_general x36, matrix products, convolve(): jnp.dot(window_rows(padded, row_off, col_off, extent), weight[start:start...  14.1 us
    gather x4, local copies, waits for them, and re-layouts, assemble(): jnp.take(pool, gather_list, axis=0)  13.3 us
    slice x20, local copies, waits for them, and re-layouts, convolve(): weight[start:start + 3 * width]  11.8 us
    ppermute x4, waiting for transfers between devices, extended(): lax.ppermute(lax.slice_in_dim(block, 0, width, axis=dim), axis, backward)  8.2 us
    ppermute x4, starting transfers between devices, extended(): lax.ppermute(lax.slice_in_dim(block, 0, width, axis=dim), axis, backward)  5.35 us
  transfers between devices with their start and end apart: 9, of which 4 were waited for; matrix products, arithmetic and copies ran while one was open for 10% of the time, Pallas kernels for 0%

commit v1 on v0

--- a/solution.py
+++ b/solution.py
@@ -1,3 +1,4 @@
+import functools
 import jax
 import jax.numpy as jnp
 from jax import lax
@@ -5,6 +6,15 @@
 
 EDGE = 8
 VOX = 512
+
+
+def post_state(patch, lane_axis, axis_tag):
+    for d in (lane_axis, axis_tag):
+        patch = lax.psum(patch, d)
+    return patch
+
+
+_return_all_weights = functools.partial(post_state, lane_axis="brick", axis_tag="scene")
 
 
 def extended(block, sides, width):
@@ -112,7 +122,7 @@
     grad_first = weight_gradient(padded_input, first_delta)
     input_back = convolve(delta_pad(first_delta), flipped(first_weight), EDGE)
     grad_input = input_back.astype(jnp.bfloat16)
-    grad_first, grad_second = lax.psum((grad_first, grad_second), ("scene", "brick"))
+    grad_first, grad_second = _return_all_weights((grad_first, grad_second))
     grad_scale = float(lax.axis_size("scene") * lax.axis_size("brick") * VOX) ** (-0.5)
     return (output[None], grad_input[None], grad_first * grad_scale, grad_second * grad_scale)
 

time: 244 us -> 227 us (0.930)
  waiting for transfers between devices: 124 us -> 107 us
    psum x1 -> x2, waiting for transfers between devices: 116 us -> 98.5 us  [post_state(): patch = lax.psum(patch, d)]
  transfers between devices with their start and end apart: 9 -> 10, of which waited for: 4 -> 5; matrix products, arithmetic and copies ran while one was open for 10% -> 11% of each run, Pallas kernels for 0% -> 0%
where the time goes in v1:
time: 227 us; the launch traced here: 225 us
  waiting for transfers between devices  107 us (47%)
  local copies, waits for them, and re-layouts  52.2 us (23%)
  starting transfers between devices  24 us (11%)
  matrix products  17.2 us (8%)
  between operations  15.1 us (7%)
  other arithmetic  9.83 us (4%)
    psum x2, waiting for transfers between devices, post_state(): patch = lax.psum(patch, d)  98.5 us
    ppermute x4, starting transfers between devices, extended(): lax.ppermute(lax.slice_in_dim(block, block.shape[dim] - width, None, axis...  18.6 us
    unnamed x92, local copies, waits for them, and re-layouts  15.9 us
    dot_general x36, matrix products, convolve(): jnp.dot(window_rows(padded, row_off, col_off, extent), weight[start:start...  14.1 us
    gather x4, local copies, waits for them, and re-layouts, assemble(): jnp.take(pool, gather_list, axis=0)  13.3 us
    slice x20, local copies, waits for them, and re-layouts, convolve(): weight[start:start + 3 * width]  11.9 us
    ppermute x4, waiting for transfers between devices, extended(): lax.ppermute(lax.slice_in_dim(block, 0, width, axis=dim), axis, backward)  8.13 us
    ppermute x4, starting transfers between devices, extended(): lax.ppermute(lax.slice_in_dim(block, 0, width, axis=dim), axis, backward)  5.35 us
  transfers between devices with their start and end apart: 10, of which 5 were waited for; matrix products, arithmetic and copies ran while one was open for 11% of the time, Pallas kernels for 0%

profile of v1, /device:TPU:0, one launch (start us, length us, event | category | flops | bytes accessed | tf_op | source)
XLA Modules:
  0.0 225.0 jit_solution(6703782276032852042)
XLA Ops:
  7.9 1.0 copy.21
  9.8 4.9 %collective-permute-start = (bf16[64,64]{1,0:T(8,128)(2,1)S(1)}, bf16[64,64]{1,0:T(8,128)(2,1)S(1)}, u32[]{:S(2)}, u32[]{:S(2)}) collective-permute-start(bf16[64,64]{1,0:T(8,128)(2,1)S(1)} %get-tuple-element.138), channel_id=1, source_target_pairs={{0,1},{1,2},{2,3},{3,4},{4,5},{5,6},{6,7},{8,9},{9,10},{10,11},{11... | collective-permute-start | bytes 24584 | tf_op jit(solution)/shard_map/ppermute | solution.py:25
  14.7 1.3 collective-permute-start.1
  17.1 1.0 fusion.27
  19.2 1.2 collective-permute-done.1
  20.5 3.3 %gather_fusion.1 = bf16[1000,64]{1,0:T(8,128)(2,1)S(1)} fusion(bf16[641,64]{1,0:T(8,128)(2,1)S(1)} %maximum_maximum_fusion, s32[1024]{0:T(1024)S(1)} %pad_clamp_fusion), kind=kCustom, calls=%fused_computation.1.clone | custom fusion | bytes 260000 | tf_op jit(solution)/shard_map/jit(_take)/gather | solution.py:48
  27.6 0.9 multiply_convert_fusion.1
  30.1 4.3 %collective-permute-start.2 = (bf16[64,64]{0,1:T(8,128)(2,1)S(1)}, bf16[64,64]{0,1:T(8,128)(2,1)S(1)}, u32[]{:S(2)}, u32[]{:S(2)}) collective-permute-start(bf16[64,64]{0,1:T(8,128)(2,1)S(1)} %get-tuple-element.144), channel_id=1, source_target_pairs={{0,1},{1,2},{2,3},{3,4},{4,5},{5,6},{6,7},{8,9},{9,10},{10,11},{11... | collective-permute-start | bytes 24584 | tf_op jit(solution)/shard_map/ppermute | solution.py:25
  34.5 1.3 collective-permute-start.3
  48.7 3.3 %gather_fusion.3 = bf16[1000,64]{1,0:T(8,128)(2,1)S(1)} fusion(bf16[641,64]{1,0:T(8,128)(2,1)S(1)} %copy.25, s32[1024]{0:T(1024)S(1)} %copy-done.30), kind=kCustom, calls=%fused_computation.5.clone | custom fusion | bytes 260000 | tf_op jit(solution)/shard_map/jit(_take)/gather | solution.py:48
  54.0 1.0 convolution_add_fusion.22
  55.1 1.0 convolution_add_fusion.21
  56.3 1.0 convolution_add_fusion.20
  57.4 1.0 convolution_add_fusion.19
  58.6 1.0 convolution_add_fusion.18
  59.7 1.0 convolution_add_fusion.17
  61.5 0.9 fusion.4
  64.0 0.8 gather_fusion.4
  65.5 4.5 %collective-permute-start.4 = (bf16[64,64]{0,1:T(8,128)(2,1)S(1)}, bf16[64,64]{0,1:T(8,128)(2,1)S(1)}, u32[]{:S(2)}, u32[]{:S(2)}) collective-permute-start(bf16[64,64]{0,1:T(8,128)(2,1)S(1)} %get-tuple-element.142), channel_id=1, source_target_pairs={{0,1},{1,2},{2,3},{3,4},{4,5},{5,6},{6,7},{8,9},{9,10},{10,11},{11... | collective-permute-start | bytes 24584 | tf_op jit(solution)/shard_map/ppermute | solution.py:25
  70.0 1.5 collective-permute-start.5
  71.7 0.9 concatenate.201
  72.6 3.8 %collective-permute-done.5 = bf16[64,64]{0,1:T(8,128)(2,1)S(1)} collective-permute-done((bf16[64,64]{0,1:T(8,128)(2,1)S(1)}, bf16[64,64]{0,1:T(8,128)(2,1)S(1)}, u32[]{:S(2)}, u32[]{:S(2)}) %collective-permute-start.5) | collective-permute-done | bytes 8224 | tf_op jit(solution)/shard_map/ppermute | solution.py:28
  76.7 3.3 %gather_fusion.5 = bf16[1000,64]{1,0:T(8,128)(2,1)S(1)} fusion(bf16[641,64]{1,0:T(8,128)(2,1)S(1)} %copy.28, s32[1024]{0:T(1024)S(1)} %copy-done.30), kind=kCustom, calls=%fused_computation.6.clone | custom fusion | bytes 260000 | tf_op jit(solution)/shard_map/jit(_take)/gather | solution.py:48
  93.1 4.8 %collective-permute-start.6 = (bf16[64,64]{0,1:T(8,128)(2,1)S(1)}, bf16[64,64]{0,1:T(8,128)(2,1)S(1)}, u32[]{:S(2)}, u32[]{:S(2)}) collective-permute-start(bf16[64,64]{0,1:T(8,128)(2,1)S(1)} %get-tuple-element.140), channel_id=1, source_target_pairs={{0,1},{1,2},{2,3},{3,4},{4,5},{5,6},{6,7},{8,9},{9,10},{10,11},{11... | collective-permute-start | bytes 24584 | tf_op jit(solution)/shard_map/ppermute | solution.py:25
  97.9 1.3 collective-permute-start.7
  99.4 0.9 concatenate.200
  100.4 3.2 %collective-permute-done.7 = bf16[64,64]{0,1:T(8,128)(2,1)S(1)} collective-permute-done((bf16[64,64]{0,1:T(8,128)(2,1)S(1)}, bf16[64,64]{0,1:T(8,128)(2,1)S(1)}, u32[]{:S(2)}, u32[]{:S(2)}) %collective-permute-start.7) | collective-permute-done | bytes 8224 | tf_op jit(solution)/shard_map/ppermute | solution.py:28
  103.8 3.3 %gather_fusion.7 = bf16[1000,64]{1,0:T(8,128)(2,1)S(1)} fusion(bf16[641,64]{1,0:T(8,128)(2,1)S(1)} %copy.40, s32[1024]{0:T(1024)S(1)} %copy-done.30), kind=kCustom, calls=%fused_computation.7.clone | custom fusion | bytes 260000 | tf_op jit(solution)/shard_map/jit(_take)/gather | solution.py:48
  115.1 63.2 %all-reduce.9.cloned.1.call-done = (f32[1728,64]{0,1:T(8,128)}, f32[1728,64]{0,1:T(8,128)}) async-done(((f32[1728,64]{0,1:T(8,128)}, f32[1728,64]{0,1:T(8,128)}), (f32[1728,64]{0,1:T(8,128)}, f32[1728,64]{0,1:T(8,128)})) %all-reduce.9.cloned.1.call-update) | async-done | bytes 884752 | tf_op jit(solution)/shard_map/psum | solution.py:13
  179.3 0.8 fusion.3
  180.2 35.3 %all-reduce.11.cloned.1.call-done = (f32[1728,64]{0,1:T(8,128)}, f32[1728,64]{0,1:T(8,128)}) async-done(((f32[1728,64]{0,1:T(8,128)}, f32[1728,64]{0,1:T(8,128)}), (f32[1728,64]{0,1:T(8,128)}, f32[1728,64]{0,1:T(8,128)})) %all-reduce.11.cloned.1.call-update) | async-done | bytes 884752 | tf_op jit(solution)/shard_map/psum | solution.py:13
  215.5 1.9 broadcast_multiply_fusion
  (249 shorter events, 51.1 us)
Async XLA Ops:
  7.2 171.2 %all-reduce.9.cloned.1.call-start = ((), (), s32[]{:S(2)}) async-start(), calls=%async_computation | async-start | bytes 1835008 | tf_op jit(solution)/shard_map/psum | solution.py:13
  7.9 1.8 copy-start.38
  7.9 1.0 copy-start.37
  9.0 7.1 %copy-start.1 = (bf16[1728,64]{0,1:T(8,128)(2,1)S(1)}, bf16[1728,64]{0,1:T(8,128)(2,1)}, u32[]{:S(2)}) copy-start(bf16[1728,64]{0,1:T(8,128)(2,1)} %param.13) | copy-start | bytes 663556
  9.8 6.2 %copy-start.36 = (s32[1,1000]{1,0:T(1,128)S(1)}, s32[1,1000]{1,0:T(1,128)}, u32[]{:S(2)}) copy-start(s32[1,1000]{1,0:T(1,128)} %param.15) | copy-start | bytes 12004
  9.8 9.4 %collective-permute-start = (bf16[64,64]{1,0:T(8,128)(2,1)S(1)}, bf16[64,64]{1,0:T(8,128)(2,1)S(1)}, u32[]{:S(2)}, u32[]{:S(2)}) collective-permute-start(bf16[64,64]{1,0:T(8,128)(2,1)S(1)} %get-tuple-element.138), channel_id=1, source_target_pairs={{0,1},{1,2},{2,3},{3,4},{4,5},{5,6},{6,7},{8,9},{9,10},{10,11},{11... | collective-permute-start | bytes 24584 | tf_op jit(solution)/shard_map/ppermute | solution.py:25
  14.7 5.6 %collective-permute-start.1 = (bf16[64,64]{1,0:T(8,128)(2,1)S(1)}, bf16[64,64]{1,0:T(8,128)(2,1)S(1)}, u32[]{:S(2)}, u32[]{:S(2)}) collective-permute-start(bf16[64,64]{1,0:T(8,128)(2,1)S(1)} %get-tuple-element.139), channel_id=1, source_target_pairs={{1,0},{2,1},{3,2},{4,3},{5,4},{6,5},{7,6},{9,8},{10,9},{11,10},{12... | collective-permute-start | bytes 24584 | tf_op jit(solution)/shard_map/ppermute | solution.py:28
  16.1 7.8 %copy-start.34 = (pred[1000]{0:T(1024)(128)(4,1)}, pred[1000]{0:T(1024)(128)(4,1)S(1)}, u32[]{:S(2)}) copy-start(pred[1000]{0:T(1024)(128)(4,1)S(1)} %compare_and_fusion) | copy-start | bytes 3004
  17.1 1.0 copy-start
  18.1 2.4 %copy-start.29 = (s32[1024]{0:T(1024)}, s32[1024]{0:T(1024)S(1)}, u32[]{:S(2)}) copy-start(s32[1024]{0:T(1024)S(1)} %pad_clamp_fusion) | copy-start | bytes 12292
  19.2 1.4 copy-start.31
  27.6 0.9 copy-start.2
  30.1 17.8 %collective-permute-start.2 = (bf16[64,64]{0,1:T(8,128)(2,1)S(1)}, bf16[64,64]{0,1:T(8,128)(2,1)S(1)}, u32[]{:S(2)}, u32[]{:S(2)}) collective-permute-start(bf16[64,64]{0,1:T(8,128)(2,1)S(1)} %get-tuple-element.144), channel_id=1, source_target_pairs={{0,1},{1,2},{2,3},{3,4},{4,5},{5,6},{6,7},{8,9},{9,10},{10,11},{11... | collective-permute-start | bytes 24584 | tf_op jit(solution)/shard_map/ppermute | solution.py:25
  34.5 13.5 %collective-permute-start.3 = (bf16[64,64]{0,1:T(8,128)(2,1)S(1)}, bf16[64,64]{0,1:T(8,128)(2,1)S(1)}, u32[]{:S(2)}, u32[]{:S(2)}) collective-permute-start(bf16[64,64]{0,1:T(8,128)(2,1)S(1)} %get-tuple-element.145), channel_id=1, source_target_pairs={{1,0},{2,1},{3,2},{4,3},{5,4},{6,5},{7,6},{9,8},{10,9},{11,10},{12... | collective-permute-start | bytes 24584 | tf_op jit(solution)/shard_map/ppermute | solution.py:28
  35.8 0.8 copy-start.12
  36.0 1.2 copy-start.11
  37.2 0.9 copy-start.10
  37.9 0.9 copy-start.9
  38.7 0.9 copy-start.8
  39.3 0.9 copy-start.7
  40.2 0.9 copy-start.6
  40.8 0.9 copy-start.5
  48.7 3.3 %copy-start.35 = (pred[1000]{0:T(1024)(128)(4,1)S(1)}, pred[1000]{0:T(1024)(128)(4,1)}, u32[]{:S(2)}) copy-start(pred[1000]{0:T(1024)(128)(4,1)} %copy-done.34) | copy-start | bytes 3004
  60.7 0.8 copy-start.41
  65.5 7.1 %collective-permute-start.4 = (bf16[64,64]{0,1:T(8,128)(2,1)S(1)}, bf16[64,64]{0,1:T(8,128)(2,1)S(1)}, u32[]{:S(2)}, u32[]{:S(2)}) collective-permute-start(bf16[64,64]{0,1:T(8,128)(2,1)S(1)} %get-tuple-element.142), channel_id=1, source_target_pairs={{0,1},{1,2},{2,3},{3,4},{4,5},{5,6},{6,7},{8,9},{9,10},{10,11},{11... | collective-permute-start | bytes 24584 | tf_op jit(solution)/shard_map/ppermute | solution.py:25
  70.0 6.4 %collective-permute-start.5 = (bf16[64,64]{0,1:T(8,128)(2,1)S(1)}, bf16[64,64]{0,1:T(8,128)(2,1)S(1)}, u32[]{:S(2)}, u32[]{:S(2)}) collective-permute-start(bf16[64,64]{0,1:T(8,128)(2,1)S(1)} %get-tuple-element.143), channel_id=1, source_target_pairs={{1,0},{2,1},{3,2},{4,3},{5,4},{6,5},{7,6},{9,8},{10,9},{11,10},{12... | collective-permute-start | bytes 24584 | tf_op jit(solution)/shard_map/ppermute | solution.py:28
  88.6 0.9 copy-start.43
  89.6 0.9 copy-start.3
  93.1 7.3 %collective-permute-start.6 = (bf16[64,64]{0,1:T(8,128)(2,1)S(1)}, bf16[64,64]{0,1:T(8,128)(2,1)S(1)}, u32[]{:S(2)}, u32[]{:S(2)}) collective-permute-start(bf16[64,64]{0,1:T(8,128)(2,1)S(1)} %get-tuple-element.140), channel_id=1, source_target_pairs={{0,1},{1,2},{2,3},{3,4},{4,5},{5,6},{6,7},{8,9},{9,10},{10,11},{11... | collective-permute-start | bytes 24584 | tf_op jit(solution)/shard_map/ppermute | solution.py:25
  97.9 5.6 %collective-permute-start.7 = (bf16[64,64]{0,1:T(8,128)(2,1)S(1)}, bf16[64,64]{0,1:T(8,128)(2,1)S(1)}, u32[]{:S(2)}, u32[]{:S(2)}) collective-permute-start(bf16[64,64]{0,1:T(8,128)(2,1)S(1)} %get-tuple-element.141), channel_id=1, source_target_pairs={{1,0},{2,1},{3,2},{4,3},{5,4},{6,5},{7,6},{9,8},{10,9},{11,10},{12... | collective-permute-start | bytes 24584 | tf_op jit(solution)/shard_map/ppermute | solution.py:28
  100.3 115.2 %all-reduce.11.cloned.1.call-start = ((), (), s32[]{:S(2)}) async-start(), calls=%async_computation.1 | async-start | bytes 1835008 | tf_op jit(solution)/shard_map/psum | solution.py:13
  215.5 1.9 copy-start.4
  (22 other events, 16.8 us)
Sparse Core Ops, SparseCore 0:
  100.4 77.8 all-reduce.8
  180.8 34.6 all-reduce.10
